TPU v7x, 128 devices: a whole 4x4x4 slice. The times are simulated.
128 devices in a mesh: dp: 16 (over z, x), member: 8 (over y, core).
Axes of the slice: x: 4, y: 4, z: 4, core: 2. Of those that a mesh axis runs over, the one named last changes fastest.
Arguments:
- fixed_rows: bfloat16 [131072, 2048], P(('dp', 'member')), may hold values from -600 to 600
- member_rows: bfloat16 [131072, 256], P(('dp', 'member')), may hold values from -0.375 to 0.375
- target: float32 [131072], P(('dp', 'member')), may hold values from -6 to 6
- fixed_prev: bfloat16 [2048], replicated, may hold values from -0.59765625 to 0.59765625
- member_id: int32 [131072], P(('dp', 'member')), may hold values from 0 to 511, as said below
Outputs:
- fixed_coef: float32 [2048], replicated
- member_coef: float32 [512, 256], P(('dp', 'member'))
- row_scores: float32 [131072], P(('dp', 'member'))
Inputs may be any that keep to these rules, and one draw needn't show every extreme that they name: `member_id`: member m belongs to owner m // 4, the device of that index along dp+member, which holds its row of member_coef. Among the 1024 rows of one device (aligned blocks) at most 24 have members of one owner; in every draw one owner gets exactly 24 rows from every device.
All inputs are finite; a program needn't handle non-finite values.
Results may differ from a plain program's by a relative error of at most 0.006.
Values may be sent and summed in bfloat16 or wider, within the bound.
No kernel may reach another device: no remote copies, remote signals or barrier semaphores. Data moves between devices by JAX's collectives and lax.ppermute only.
A program may use at most 192 MiB of HBM per device.

v0:
```python
import jax
import jax.numpy as jnp
from jax import lax
from jax.sharding import PartitionSpec as P

MEM_DEV = 4


RIDGE_FIXED = 4.0
RIDGE_MEMBER = 1.0


def block_solve(matrix, right_side):
    order = matrix.shape[0]
    width = min(512, order)
    count = order // width
    hold = lax.Precision.HIGHEST
    eye_block = jnp.eye(width, dtype=jnp.float32)
    inverses = []
    panels = []
    work = matrix
    for step in range(count):
        lo = step * width
        hi = lo + width
        factor_blk = jnp.linalg.cholesky(work[lo:hi, lo:hi])
        inverse_blk = jax.scipy.linalg.solve_triangular(factor_blk, eye_block, lower=True)
        inverses.append(inverse_blk)
        if step + 1 < count:
            panel = jnp.dot(work[hi:, lo:hi], inverse_blk.T, precision=hold)
            panels.append(panel)
            work = work.at[hi:, hi:].add(-jnp.dot(panel, panel.T, precision=hold))
    forward = []
    for step in range(count):
        lo = step * width
        partial_rhs = right_side[lo : lo + width]
        for prior in range(step):
            lower_blk = panels[prior][(step - prior - 1) * width : (step - prior) * width]
            partial_rhs = partial_rhs - jnp.dot(lower_blk, forward[prior], precision=hold)
        forward.append(jnp.dot(inverses[step], partial_rhs, precision=hold))
    backward = [None] * count
    for step in range(count - 1, -1, -1):
        partial_rhs = forward[step]
        for later in range(step + 1, count):
            lower_blk = panels[step][(later - step - 1) * width : (later - step) * width]
            partial_rhs = partial_rhs - jnp.dot(lower_blk.T, backward[later], precision=hold)
        backward[step] = jnp.dot(inverses[step].T, partial_rhs, precision=hold)
    return jnp.concatenate(backward, axis=0)


def solve_members(recv_rows, recv_resid, recv_hot):
    mem_width = recv_rows.shape[1]
    weighted = recv_hot[:, :, None] * recv_rows[:, None, :]
    member_gram = jnp.einsum("smd,se->mde", weighted, recv_rows, preferred_element_type=jnp.float32)
    member_rhs = jnp.einsum(
        "sm,sd->md", recv_hot * recv_resid[:, None], recv_rows, preferred_element_type=jnp.float32
    )
    member_coef = jax.vmap(block_solve)(
        member_gram + RIDGE_MEMBER * jnp.eye(mem_width, dtype=jnp.float32), member_rhs
    )
    member_low = member_coef.astype(jnp.bfloat16)
    projected = jnp.dot(recv_rows, member_low.T, preferred_element_type=jnp.float32)
    slot_score = jnp.sum(projected * recv_hot.astype(jnp.float32), axis=1)
    return (member_coef, slot_score)


def shards(fixed_rows, member_rows, target, fixed_prev, member_id):
    row_count, fix_width = fixed_rows.shape
    mem_width = member_rows.shape[1]
    devices = lax.axis_size(("dp", "member"))
    capacity = 3 * row_count // devices
    prior_score = jnp.dot(fixed_rows, fixed_prev, preferred_element_type=jnp.float32)
    member_resid = (target - prior_score).astype(jnp.bfloat16)
    owner_ids = member_id // MEM_DEV
    local_ids = member_id % MEM_DEV
    owner_hot = (owner_ids[:, None] == jnp.arange(devices, dtype=jnp.int32)[None, :]).astype(
        jnp.int32
    )
    position = jnp.sum((jnp.cumsum(owner_hot, axis=0) - 1) * owner_hot, axis=1)
    slot_index = owner_ids * capacity + position
    member_hot = (local_ids[:, None] == jnp.arange(MEM_DEV, dtype=jnp.int32)[None, :]).astype(
        jnp.bfloat16
    )
    send_rows = (
        jnp.zeros((devices * capacity, mem_width), jnp.bfloat16).at[slot_index].set(member_rows)
    )
    send_resid = jnp.zeros((devices * capacity,), jnp.bfloat16).at[slot_index].set(member_resid)
    send_hot = jnp.zeros((devices * capacity, MEM_DEV), jnp.bfloat16).at[slot_index].set(member_hot)
    received = (
        lax.all_to_all(
            send_rows.reshape(devices, capacity, mem_width),
            ("dp", "member"),
            split_axis=0,
            concat_axis=0,
            tiled=True,
        ),
        lax.all_to_all(
            send_resid.reshape(devices, capacity),
            ("dp", "member"),
            split_axis=0,
            concat_axis=0,
            tiled=True,
        ),
        lax.all_to_all(
            send_hot.reshape(devices, capacity, MEM_DEV),
            ("dp", "member"),
            split_axis=0,
            concat_axis=0,
            tiled=True,
        ),
    )
    recv_rows = received[0].reshape(devices * capacity, mem_width)
    recv_resid = received[1].reshape(devices * capacity)
    recv_hot = received[2].reshape(devices * capacity, MEM_DEV)
    member_coef, slot_score = solve_members(recv_rows, recv_resid, recv_hot)
    returned = lax.all_to_all(
        slot_score.reshape(devices, capacity),
        ("dp", "member"),
        split_axis=0,
        concat_axis=0,
        tiled=True,
    )
    member_score = returned.reshape(devices * capacity)[slot_index]
    fixed_resid = (target - member_score).astype(jnp.bfloat16)
    gradient = lax.psum(
        jnp.dot(fixed_resid, fixed_rows, preferred_element_type=jnp.float32), ("dp", "member")
    )
    gram_share = lax.psum_scatter(
        lax.dot_general(
            fixed_rows, fixed_rows, (((0,), (0,)), ((), ())), preferred_element_type=jnp.float32
        ),
        ("dp", "member"),
        scatter_dimension=0,
        tiled=True,
    )
    gram_whole = lax.all_gather(gram_share, ("dp", "member"), axis=0, tiled=True)
    fixed_coef = block_solve(
        gram_whole + RIDGE_FIXED * jnp.eye(fix_width, dtype=jnp.float32), gradient
    )
    row_scores = (
        jnp.dot(fixed_rows, fixed_coef.astype(jnp.bfloat16), preferred_element_type=jnp.float32)
        + member_score
    )
    return (fixed_coef, member_coef, row_scores)


def solution(mesh):
    placed = (
        P(("dp", "member"), None),
        P(("dp", "member"), None),
        P(("dp", "member")),
        P(),
        P(("dp", "member")),
    )
    return jax.shard_map(
        shards,
        mesh=mesh,
        in_specs=placed,
        out_specs=(P(), P(("dp", "member"), None), P(("dp", "member"))),
        check_vma=False,
    )
```

profile of v0, /device:TPU:1, one launch (start us, length us, event | category | flops | bytes accessed | tf_op | source)
XLA Modules:
  0.0 1895.1 jit_solution(11088358401950788135)
XLA Ops:
  7.2 15.2 fusion.241
  22.5 661.5 %reduce-scatter.4.cloned.1.call-done = f32[16,2048]{1,0:T(8,128)} async-done(((f32[2048,2048]{1,0:T(8,128)}), f32[16,2048]{1,0:T(8,128)}) %reduce-scatter.4.cloned.1.call-update) | async-done | bytes 131088 | tf_op jit(solution)/shard_map/reduce_scatter | solution.py:127
  697.3 11.6 all-to-all-start.2
  745.4 37.3 %all-to-all-done = bf16[128,24,256]{2,1,0:T(8,128)(2,1)S(1)} async-done(((bf16[128,24,256]{2,1,0:T(8,128)(2,1)}), bf16[128,24,256]{2,1,0:T(8,128)(2,1)S(1)}, u32[]{:S(2)}, u32[]{:S(2)}) %all-to-all-start) | async-done | bytes 1572896 | tf_op jit(solution)/shard_map/all_to_all | solution.py:89
  794.1 46.9 %custom-call.40 = f32[4,128,128]{2,1,0:T(8,128)S(1)} custom-call(f32[4,128,128]{2,1,0:T(8,128)S(1)} %cholesky.881), custom_call_target="Cholesky" | custom-call | tf_op jit(solution)/shard_map/vmap(jit(cholesky))/cholesky | solution.py:25
  842.2 39.9 %custom-call.41 = f32[4,1,128,128]{2,3,1,0:T(8,128)} custom-call(f32[4,1,128,128]{3,2,1,0:T(8,128)S(1)} %select_bitcast_fusion), custom_call_target="InvertDiagBlocksLowerTriangular" | custom-call | tf_op jit(solution)/shard_map/vmap(jit(cholesky))/cholesky | solution.py:25
  886.6 47.9 %custom-call.42 = f32[4,128,128]{2,1,0:T(8,128)S(1)} custom-call(f32[4,128,128]{2,1,0:T(8,128)} %convolution_subtract_fusion.7), custom_call_target="Cholesky" | custom-call | tf_op jit(solution)/shard_map/vmap(jit(cholesky))/cholesky | solution.py:25
  945.5 79.4 %custom-call.43 = f32[4,2,128,128]{2,3,1,0:T(8,128)S(1)} custom-call(f32[4,2,128,128]{3,2,1,0:T(8,128)} %bitcast.423), custom_call_target="InvertDiagBlocksLowerTriangular" | custom-call | tf_op jit(solution)/shard_map/vmap(jit(_solve_triangular))/triangular_solve | solution.py:26
  1055.2 62.8 %psum.7 = f32[2048]{0:T(1024)S(1)} all-reduce(f32[2048]{0:T(1024)S(1)} %bitcast.392), channel_id=1, replica_groups=mesh['dp'=16,'member'=8] {'dp','member'}, use_global_device_ids=true, to_apply=%region_20.23 | all-reduce | flops 2048 | bytes 16384 | tf_op jit(solution)/shard_map/psum | solution.py:124
  1118.0 17.6 copy.93
  1150.8 11.7 cholesky.584
  1162.5 9.8 custom-call.56
  1173.1 11.7 cholesky.603
  1184.9 10.0 custom-call.57
  1195.5 11.7 cholesky.624
  1207.9 9.8 custom-call.58
  1218.3 11.7 cholesky.641
  1243.2 39.3 %custom-call.59 = f32[4,128,128]{1,2,0:T(8,128)S(1)} custom-call(f32[4,128,128]{2,1,0:T(8,128)S(1)} %get-tuple-element.75), custom_call_target="InvertDiagBlocksLowerTriangular" | custom-call | tf_op jit(solution)/shard_map/jit(_solve_triangular)/triangular_solve | solution.py:26
  1289.4 12.1 fusion.2
  1301.6 17.1 slice_add_fusion
  1330.8 11.7 cholesky.656
  1344.2 10.2 custom-call.60
  1358.3 11.7 cholesky.675
  1372.7 9.8 custom-call.61
  1386.4 13.3 cholesky.696
  1401.9 11.3 custom-call.62
  1416.2 11.7 cholesky.713
  1434.8 13.6 while.14
  1448.5 40.9 %custom-call.63 = f32[4,128,128]{1,2,0:T(8,128)} custom-call(f32[4,128,128]{2,1,0:T(8,128)} %get-tuple-element.76), custom_call_target="InvertDiagBlocksLowerTriangular" | custom-call | tf_op jit(solution)/shard_map/jit(_solve_triangular)/triangular_solve | solution.py:26
  1506.3 10.0 slice_add_fusion.1
  1526.9 11.7 cholesky.728
  1540.3 9.8 custom-call.64
  1554.0 11.9 cholesky.747
  1568.5 9.8 custom-call.65
  1582.3 13.2 cholesky.768
  1597.6 11.3 custom-call.66
  1611.9 12.1 cholesky.785
  1630.9 13.9 while.15
  1644.8 40.7 %custom-call.67 = f32[4,128,128]{1,2,0:T(8,128)} custom-call(f32[4,128,128]{2,1,0:T(8,128)} %get-tuple-element.77), custom_call_target="InvertDiagBlocksLowerTriangular" | custom-call | tf_op jit(solution)/shard_map/jit(_solve_triangular)/triangular_solve | solution.py:26
  1708.6 11.9 cholesky.800
  1722.1 9.8 custom-call.68
  1735.8 11.7 cholesky.819
  1750.1 9.8 custom-call.69
  1763.8 13.4 cholesky.840
  1779.3 11.3 custom-call.70
  1793.7 11.7 cholesky.857
  1812.4 13.9 while.16
  1826.3 41.0 %custom-call.71 = f32[4,128,128]{1,2,0:T(8,128)} custom-call(f32[4,128,128]{2,1,0:T(8,128)} %get-tuple-element.78), custom_call_target="InvertDiagBlocksLowerTriangular" | custom-call | tf_op jit(solution)/shard_map/jit(_solve_triangular)/triangular_solve | solution.py:26
  (406 shorter events, 347.3 us)
Async XLA Ops:
  7.2 676.8 %reduce-scatter.4.cloned.1.call-start = ((), (), s32[]{:S(2)}) async-start(), calls=%async_computation.6 | async-start | bytes 16908288 | tf_op jit(solution)/shard_map/reduce_scatter | solution.py:127
  22.4 661.6 %copy-start.59 = (s32[1024]{0:T(1024)S(1)}, s32[1024]{0:T(1024)}, u32[]{:S(2)}) copy-start(s32[1024]{0:T(1024)} %param.18) | copy-start | bytes 12292
  22.4 662.1 %copy-start.60 = (bf16[2048]{0:T(1024)(128)(2,1)S(1)}, bf16[2048]{0:T(1024)(128)(2,1)}, u32[]{:S(2)}) copy-start(bf16[2048]{0:T(1024)(128)(2,1)} %param.17) | copy-start | bytes 12292
  22.4 1095.5 %all-gather.2.cloned.1.call-start = ((), (), s32[]{:S(2)}) async-start(), calls=%async_computation.5 | async-start | bytes 16908288 | tf_op jit(solution)/shard_map/all_gather | solution.py:135
  684.6 3.8 copy-start.53
  697.3 21.4 %all-to-all-start.2 = ((bf16[128,1,24]{2,1,0:T(2,128)(2,1)}), bf16[128,1,24]{2,1,0:T(2,128)(2,1)S(1)}, u32[]{:S(2)}, u32[]{:S(2)}) async-start(bf16[128,1,24]{2,1,0:T(2,128)(2,1)} %all_to_all.24), calls=%async_computation.2 | async-start | bytes 131072 | tf_op jit(solution)/shard_map/all_to_all | solution.py:96
  718.6 15.9 all-to-all-start.1
  734.5 48.2 %all-to-all-start = ((bf16[128,24,256]{2,1,0:T(8,128)(2,1)}), bf16[128,24,256]{2,1,0:T(8,128)(2,1)S(1)}, u32[]{:S(2)}, u32[]{:S(2)}) async-start(bf16[128,24,256]{2,1,0:T(8,128)(2,1)} %bitcast.387), calls=%async_computation | async-start | bytes 3145728 | tf_op jit(solution)/shard_map/all_to_all | solution.py:89
  743.3 543.4 %copy-start.6 = (f32[512,512]{1,0:T(8,128)}, f32[512,512]{1,0:T(8,128)S(1)}, u32[]{:S(2)}) copy-start(f32[512,512]{1,0:T(8,128)S(1)} %fusion.38) | copy-start | bytes 3145732
  745.4 39.1 %copy-start.44 = (bf16[3072,4]{0,1:T(4,128)(2,1)S(1)}, bf16[3072,4]{0,1:T(4,128)(2,1)}, u32[]{:S(2)}) copy-start(bf16[3072,4]{0,1:T(4,128)(2,1)} %mul.49) | copy-start | bytes 73732
  791.4 50.8 %copy-start.47 = (pred[128,128]{1,0:T(8,128)(4,1)S(1)}, pred[128,128]{1,0:T(8,128)(4,1)}, u32[]{:S(2)}) copy-start(pred[128,128]{1,0:T(8,128)(4,1)} %iota_compare_fusion.10) | copy-start | bytes 49156
  794.1 140.4 %copy-start.46 = (pred[128,128]{1,0:T(8,128)(4,1)S(1)}, pred[128,128]{1,0:T(8,128)(4,1)}, u32[]{:S(2)}) copy-start(pred[128,128]{1,0:T(8,128)(4,1)} %iota_compare_fusion.11) | copy-start | bytes 49156
  935.3 90.3 %copy-start.41 = (f32[128,256]{1,0:T(8,128)S(1)}, f32[128,256]{1,0:T(8,128)}, u32[]{:S(2)}) copy-start(f32[128,256]{1,0:T(8,128)} %get-tuple-element.135) | copy-start | bytes 393220
  1025.5 4.4 copy-start.45
  1027.8 18.4 copy-start.54
  1029.9 25.3 %copy-start.52 = (f32[4,1,256]{2,0,1:T(4,128)}, f32[4,1,256]{2,0,1:T(4,128)S(1)}, u32[]{:S(2)}) copy-start(f32[4,1,256]{2,0,1:T(4,128)S(1)} %copy.167) | copy-start | bytes 12292
  1031.1 13.6 all-to-all-start.3
  1117.9 17.6 copy-start.49
  1143.1 5.7 copy-start
  1284.1 17.4 copy-start.1
  1284.6 34.1 %copy-start.15 = (f32[128,512]{1,0:T(8,128)}, f32[128,512]{1,0:T(8,128)S(1)}, u32[]{:S(2)}) copy-start(f32[128,512]{1,0:T(8,128)S(1)} %fusion.174) | copy-start | bytes 786436
  1286.6 32.1 %copy-start.26 = (f32[128,512]{1,0:T(8,128)}, f32[128,512]{1,0:T(8,128)S(1)}, u32[]{:S(2)}) copy-start(f32[128,512]{1,0:T(8,128)S(1)} %fusion.172) | copy-start | bytes 786436
  1289.4 29.3 %copy-start.32 = (f32[128,512]{1,0:T(8,128)}, f32[128,512]{1,0:T(8,128)S(1)}, u32[]{:S(2)}) copy-start(f32[128,512]{1,0:T(8,128)S(1)} %fusion.171) | copy-start | bytes 786436
  1301.6 17.2 slice-start
  1318.7 5.8 copy-start.5
  1489.4 5.7 copy-start.43
  1490.9 25.4 %copy-start.11 = (f32[128,512]{1,0:T(8,128)}, f32[128,512]{1,0:T(8,128)S(1)}, u32[]{:S(2)}) copy-start(f32[128,512]{1,0:T(8,128)S(1)} %fusion.116) | copy-start | bytes 786436
  1493.6 22.7 %copy-start.17 = (f32[128,512]{1,0:T(8,128)}, f32[128,512]{1,0:T(8,128)S(1)}, u32[]{:S(2)}) copy-start(f32[128,512]{1,0:T(8,128)S(1)} %fusion.168) | copy-start | bytes 786436
  1495.6 20.7 %copy-start.28 = (f32[128,512]{1,0:T(8,128)}, f32[128,512]{1,0:T(8,128)S(1)}, u32[]{:S(2)}) copy-start(f32[128,512]{1,0:T(8,128)S(1)} %fusion.166) | copy-start | bytes 786436
  1497.8 18.5 copy-start.34
  1506.2 12.7 copy-start.2
  1506.3 10.0 copy-start.50
  1516.3 4.2 copy-start.9
  1685.6 10.2 copy-start.10
  1687.1 12.2 copy-start.13
  1689.8 9.5 copy-start.19
  1826.3 49.3 %copy-start.51 = (f32[2048]{0:T(1024)S(1)}, f32[2048]{0:T(1024)}, u32[]{:S(2)}) copy-start(f32[2048]{0:T(1024)} %copy-done.49) | copy-start | bytes 24580
  1826.3 49.3 %copy-start.57 = (f32[1,512]{1,0:T(1,128)S(1)}, f32[1,512]{1,0:T(1,128)}, u32[]{:S(2)}) copy-start(f32[1,512]{1,0:T(1,128)} %fusion.46) | copy-start | bytes 6148
  1826.3 49.3 %copy-start.58 = (f32[1,512]{1,0:T(1,128)S(1)}, f32[1,512]{1,0:T(1,128)}, u32[]{:S(2)}) copy-start(f32[1,512]{1,0:T(1,128)} %fusion.48) | copy-start | bytes 6148
  1867.3 5.8 copy-start.42
  1867.3 8.3 copy-start.14
  1867.3 8.3 copy-start.20
  1867.3 8.3 copy-start.31
  1867.3 8.3 copy-start.37
  1870.2 6.5 copy-start.8
  1871.5 6.1 copy-start.55
  1871.6 6.1 copy-start.56
  1882.0 4.0 copy-start.4
  (20 other events, 44.3 us)
Sparse Core Ops, SparseCore 0:
  22.5 661.3 reduce-scatter.3
  687.1 99.4 all-gather.1
where the time goes:
time: 1910 us; the launch traced here: 1900 us
  other arithmetic  750 us (39%)
  waiting for transfers between devices  716 us (37%)
  matrix products  174 us (9%)
  local copies, waits for them, and re-layouts  138 us (7%)
  blocking collectives  62.8 us (3%)
  starting transfers between devices  27.8 us (1%)
  between operations  26.2 us (1%)
    reduce_scatter x1, waiting for transfers between devices, shards(): lax.psum_scatter(lax.dot_general(fixed_rows, fixed_rows, (((0,), (0,)), (...  662 us
    another operation x69, other arithmetic, block_solve(): factor_blk = jnp.linalg.cholesky(work[lo:hi, lo:hi])  474 us
    another operation x13, other arithmetic, block_solve(): jax.scipy.linalg.solve_triangular(factor_blk, eye_block, lower=True)  252 us
    psum x1, blocking collectives, shards(): lax.psum(jnp.dot(fixed_resid, fixed_rows, preferred_element_type=jnp.floa...  62.8 us
    another operation x55, local copies, waits for them, and re-layouts, block_solve(): jax.scipy.linalg.solve_triangular(factor_blk, eye_block, lower=True)  52 us
  transfers between devices with their start and end apart: 6, of which 5 were waited for; matrix products, arithmetic and copies ran while one was open for 15% of the time, Pallas kernels for 0%

commit v1 on v0

v1 whole, which is shorter than its diff:
```python
import functools

import jax
import jax.numpy as jnp
from jax import lax
from jax.experimental import pallas as pl
from jax.experimental.pallas import tpu as pltpu
from jax.sharding import Mesh
from jax.sharding import PartitionSpec as P

F32 = jnp.float32
BF16 = jnp.bfloat16
HIGH = lax.Precision.HIGHEST
ALL = ("z", "x", "y", "core")
CHIPS = ("z", "x", "y")

MEM_DEV = 4
RIDGE_FIXED = 4.0
RIDGE_MEMBER = 1.0
GROUP = 1

FIX = 2048
MEM = 256
PAY = 384
BLK = 256
NBLK = FIX // BLK
CORE_PAIRS = 18


def pair_table():
    table = []
    for core in range(2):
        pairs = []
        for i in range(4 * core, 4 * core + 4):
            pairs += [(i, (i + k) % NBLK) for k in range(4)]
        pairs += [(0, 4), (1, 5)] if core == 0 else [(6, 2), (7, 3)]
        table.append([(max(p), min(p)) for p in pairs])
    return table


def params(mb=56):
    return pltpu.CompilerParams(vmem_limit_bytes=mb << 20)


def dot_nn(a, b, precision=None):
    return lax.dot_general(a, b, (((1,), (0,)), ((), ())), precision=precision, preferred_element_type=F32)


def dot_nt(a, b, precision=None):
    return lax.dot_general(a, b, (((1,), (1,)), ((), ())), precision=precision, preferred_element_type=F32)


def dot_tn(a, b, precision=None):
    return lax.dot_general(a, b, (((0,), (0,)), ((), ())), precision=precision, preferred_element_type=F32)


def split3(v):
    hi = v.astype(BF16)
    rest = v - hi.astype(F32)
    mid = rest.astype(BF16)
    low = (rest - mid.astype(F32)).astype(BF16)
    return hi, mid, low


def over_lanes(v, c):
    return jnp.broadcast_to(v[:, c : c + 1], v.shape)


def over_rows(v, i):
    return jnp.broadcast_to(v[i : i + 1, :], v.shape)


def factor128(blocks):
    n = len(blocks)
    sub = lax.broadcasted_iota(jnp.int32, (8, 128), 0)
    lane = lax.broadcasted_iota(jnp.int32, (8, 128), 1)
    a = [[blk[8 * t : 8 * t + 8, :] for t in range(16)] for blk in blocks]
    e = [[(lane == sub + 8 * t).astype(F32) for t in range(16)] for _ in blocks]
    out = [[] for _ in blocks]
    b = [[over_lanes(a[p][0], k) for k in range(8)] for p in range(n)]
    for s in range(16):
        more = s < 15
        r = [a[p][s] for p in range(n)]
        f = [e[p][s] for p in range(n)]
        if more:
            r1 = [a[p][s + 1] for p in range(n)]
            f1 = [e[p][s + 1] for p in range(n)]
            q = [[over_lanes(r1[p], 8 * s + k) for k in range(8)] for p in range(n)]
            bn = [[over_lanes(r1[p], 8 * s + 8 + k) for k in range(8)] for p in range(n)]
        scale = [jnp.zeros((8, 128), F32) for _ in range(n)]
        for i in range(8):
            for p in range(n):
                inv = 1.0 / over_rows(b[p][i], i)
                scale[p] = jnp.where(sub == i, inv, scale[p])
                ri, fi = over_rows(r[p], i), over_rows(f[p], i)
                if i < 7:
                    m = jnp.where(sub > i, b[p][i] * inv, 0.0)
                    r[p] = r[p] - m * ri
                    f[p] = f[p] - m * fi
                bk = [None] * 8
                for k in range(i + 1, 8):
                    bk[k] = over_rows(b[p][k], i)
                    b[p][k] = b[p][k] - m * bk[k]
                if more:
                    mq = q[p][i] * inv
                    r1[p] = r1[p] - mq * ri
                    f1[p] = f1[p] - mq * fi
                    for k in range(i + 1, 8):
                        q[p][k] = q[p][k] - mq * bk[k]
                    for k in range(8):
                        bn[p][k] = bn[p][k] - mq * over_rows(q[p][i], k)
        for p in range(n):
            root = jnp.sqrt(scale[p])
            y, z = r[p] * root, f[p] * root
            out[p].append(z)
            if more:
                a[p][s + 1], e[p][s + 1] = r1[p], f1[p]
                b[p] = bn[p]
            if s < 14:
                u = dot_tn(y, jnp.concatenate([y, z], axis=1), HIGH)
                for t in range(s + 2, 16):
                    a[p][t] = a[p][t] - u[8 * t : 8 * t + 8, :128]
                    e[p][t] = e[p][t] - u[8 * t : 8 * t + 8, 128:]
    return [jnp.concatenate(o, axis=0) for o in out]


def dispatch_kernel(cap, fix_ref, prev_ref, target_ref, id_ref, rows_ref, send_ref, slot_ref):
    count = rows_ref.shape[0]
    owners = send_ref.shape[0] // cap
    prior = dot_nt(prev_ref[...], fix_ref[...])
    resid = (target_ref[...] - prior).astype(BF16)
    ids = id_ref[...]
    owner = ids // MEM_DEV
    local = ids - owner * MEM_DEV
    hot = lax.broadcasted_iota(jnp.int32, (owners, count), 0) == owner
    before = (
        lax.broadcasted_iota(jnp.int32, (count, count), 0)
        < lax.broadcasted_iota(jnp.int32, (count, count), 1)
    ).astype(BF16)
    ahead = dot_nn(hot.astype(BF16), before)
    place = jnp.sum(jnp.where(hot, ahead, 0.0), axis=0, keepdims=True)
    slot = owner * cap + place.astype(jnp.int32)
    slot_ref[...] = slot
    kind = lax.broadcasted_iota(jnp.int32, (128, count), 0)
    meta = jnp.where(
        kind == 0,
        jnp.broadcast_to(resid.astype(F32), (128, count)),
        (kind == local + 1).astype(F32),
    ).astype(BF16)
    rows = rows_ref[...]
    for c in range(owners * cap // 256):
        pick = (
            lax.broadcasted_iota(jnp.int32, (256, count), 0) + 256 * c == slot
        ).astype(BF16)
        send_ref[256 * c : 256 * c + 256, :MEM] = dot_nn(pick, rows).astype(BF16)
        send_ref[256 * c : 256 * c + 256, MEM:] = dot_nt(pick, meta).astype(BF16)


def member_kernel(recv_ref, coef_ref, score_ref, turned_ref, gram_ref, rhs_ref):
    slots = recv_ref.shape[0]
    unit = (
        lax.broadcasted_iota(jnp.int32, (PAY, PAY), 0)
        == lax.broadcasted_iota(jnp.int32, (PAY, PAY), 1)
    ).astype(BF16)
    for c in range(slots // 256):
        turned_ref[:, 256 * c : 256 * c + 256] = dot_nt(
            unit, recv_ref[256 * c : 256 * c + 256, :]
        ).astype(BF16)
    rows = recv_ref[:, :MEM]
    hots = turned_ref[MEM + 1 : MEM + 1 + MEM_DEV, :]
    resid = turned_ref[MEM : MEM + 1, :]
    rhs_ref[...] = dot_nn(hots * resid, rows)
    ridge = jnp.where(
        lax.broadcasted_iota(jnp.int32, (MEM, MEM), 0)
        == lax.broadcasted_iota(jnp.int32, (MEM, MEM), 1),
        RIDGE_MEMBER,
        0.0,
    )
    for m in range(MEM_DEV):
        gram_ref[m] = dot_nn(turned_ref[:MEM, :] * hots[m : m + 1, :], rows) + ridge

    def solve(p, carry):
        base = GROUP * p
        grams = [gram_ref[base + i] for i in range(GROUP)]
        w0 = factor128([g[:128, :128] for g in grams])
        l10 = [dot_nt(g[128:, :128], w, HIGH) for g, w in zip(grams, w0)]
        w1 = factor128([g[128:, 128:] - dot_nt(l, l, HIGH) for g, l in zip(grams, l10)])
        for i in range(GROUP):
            right = rhs_ref[pl.ds(base + i, 1), :]
            y0 = dot_nt(right[:, :128], w0[i], HIGH)
            y1 = dot_nt(right[:, 128:] - dot_nt(y0, l10[i], HIGH), w1[i], HIGH)
            x1 = dot_nn(y1, w1[i], HIGH)
            x0 = dot_nn(y0 - dot_nn(x1, l10[i], HIGH), w0[i], HIGH)
            coef_ref[pl.ds(base + i, 1), :] = jnp.concatenate([x0, x1], axis=1)
        return carry

    lax.fori_loop(0, MEM_DEV // GROUP, solve, 0)
    low = coef_ref[...].astype(BF16)
    projected = dot_nn(low, turned_ref[:MEM, :])
    score_ref[...] = jnp.sum(projected * hots.astype(F32), axis=0, keepdims=True)


def combine_kernel(back_ref, slot_ref, target_ref, score_ref, resid_ref):
    slots, count = back_ref.shape[1], slot_ref.shape[1]
    parts = split3(back_ref[...])
    stack = jnp.concatenate([part.astype(F32) for part in parts] + [jnp.zeros((5, slots), F32)], axis=0).astype(BF16)
    slot = slot_ref[...]
    total = jnp.zeros((8, count), F32)
    for c in range(slots // 256):
        pick = (
            lax.broadcasted_iota(jnp.int32, (256, count), 0) + 256 * c == slot
        ).astype(BF16)
        total = total + dot_nn(stack[:, 256 * c : 256 * c + 256], pick)
    score = total[0:1] + (total[1:2] + total[2:3])
    score_ref[...] = score
    resid_ref[...] = (target_ref[...] - score).astype(BF16)


def gram_kernel(hi_ref, lo_ref, own_i, own_j, other_i, other_j, out_ref):
    block = dot_tn(own_i[...], own_j[...]) + dot_tn(other_i[...], other_j[...])
    out_ref[:32, 0] = block[:, :128].reshape(32, 8, 128)
    out_ref[32:, 0] = block[:, 128:].reshape(32, 8, 128)


def gram_blocks(own, other, hi, lo):
    rows = own.shape[0]
    tall = lambda pick: pl.BlockSpec((rows, BLK), pick)
    return pl.pallas_call(
        gram_kernel,
        out_shape=jax.ShapeDtypeStruct((64, CORE_PAIRS, 8, 128), F32),
        grid_spec=pltpu.PrefetchScalarGridSpec(
            num_scalar_prefetch=2,
            grid=(CORE_PAIRS,),
            in_specs=[
                tall(lambda b, hi, lo: (0, hi[b])),
                tall(lambda b, hi, lo: (0, lo[b])),
                tall(lambda b, hi, lo: (0, hi[b])),
                tall(lambda b, hi, lo: (0, lo[b])),
            ],
            out_specs=pl.BlockSpec((64, 1, 8, 128), lambda b, hi, lo: (0, b, 0, 0)),
        ),
        compiler_params=params(32),
        name="gram",
    )(hi, lo, own, own, other, other)


def place_of(i, j):
    return i * (i + 1) // 2 + j


def read_block(a_ref, at):
    flat = a_ref[at].reshape(2 * BLK, 128)
    return jnp.concatenate([flat[:BLK], flat[BLK:]], axis=1)


def write_block(a_ref, at, value):
    a_ref[at] = jnp.concatenate([value[:, :128], value[:, 128:]], axis=0).reshape(64, 8, 128)


def factor_kernel(gram_ref, a_ref, w_ref, left_ref, right_ref, sems):
    copies = []
    for core, pairs in enumerate(pair_table()):
        for b, (i, j) in enumerate(pairs):
            at = place_of(i, j)
            copies.append(
                pltpu.make_async_copy(gram_ref.at[:, core, b], a_ref.at[at], sems.at[at])
            )
    for copy in copies:
        copy.start()
    for copy in copies:
        copy.wait()
    ridge = jnp.where(
        lax.broadcasted_iota(jnp.int32, (128, 128), 0)
        == lax.broadcasted_iota(jnp.int32, (128, 128), 1),
        RIDGE_FIXED,
        0.0,
    )

    def step(k, carry):
        diag = a_ref[place_of(k, k)].reshape(2 * BLK, 128)
        w00 = factor128([diag[:128] + ridge])[0]
        l10 = dot_nt(diag[128:256], w00, HIGH)
        w11 = factor128([diag[384:] + ridge - dot_nt(l10, l10, HIGH)])[0]
        w10 = -dot_nn(w11, dot_nn(l10, w00, HIGH), HIGH)
        w_ref[k, :128, :128] = w00
        w_ref[k, :128, 128:] = jnp.zeros((128, 128), F32)
        w_ref[k, 128:, :128] = w10
        w_ref[k, 128:, 128:] = w11
        whole = w_ref[k]

        def panel(i, carry):
            at = place_of(i, k)
            value = dot_nt(read_block(a_ref, at), whole, HIGH)
            write_block(a_ref, at, value)
            h, m, l = split3(value)
            left_ref[i] = jnp.concatenate([h, h, m, h, l, m], axis=1)
            right_ref[i] = jnp.concatenate([h, m, h, l, h, m], axis=1)
            return carry

        lax.fori_loop(k + 1, NBLK, panel, 0)

        def trail_row(i, carry):
            def trail(j, carry):
                at = place_of(i, j)
                gain = dot_nt(left_ref[i], right_ref[j])
                flat = jnp.concatenate([gain[:, :128], gain[:, 128:]], axis=0)
                a_ref[at] = a_ref[at] - flat.reshape(64, 8, 128)
                return carry

            return lax.fori_loop(k + 1, i + 1, trail, carry)

        return lax.fori_loop(k + 1, NBLK, trail_row, carry)

    lax.fori_loop(0, NBLK, step, 0)


def factor_fixed(gram):
    count = NBLK * (NBLK + 1) // 2
    return pl.pallas_call(
        factor_kernel,
        out_shape=(
            jax.ShapeDtypeStruct((count, 64, 8, 128), F32),
            jax.ShapeDtypeStruct((NBLK, BLK, BLK), F32),
        ),
        in_specs=[pl.BlockSpec(memory_space=pl.ANY)],
        out_specs=(
            pl.BlockSpec(memory_space=pltpu.VMEM),
            pl.BlockSpec(memory_space=pltpu.VMEM),
        ),
        scratch_shapes=[
            pltpu.VMEM((NBLK, BLK, 6 * BLK), BF16),
            pltpu.VMEM((NBLK, BLK, 6 * BLK), BF16),
            pltpu.SemaphoreType.DMA((count,)),
        ],
        compiler_params=params(),
        name="factor_fixed",
    )(gram)


def solve_kernel(a_ref, w_ref, grad_ref, fix_ref, member_ref, coef_ref, score_ref):
    forward = []
    for k in range(NBLK):
        part = grad_ref[:, BLK * k : BLK * k + BLK]
        for j in range(k):
            part = part - dot_nt(forward[j], read_block(a_ref, place_of(k, j)), HIGH)
        forward.append(dot_nt(part, w_ref[k], HIGH))
    backward = [None] * NBLK
    for k in range(NBLK - 1, -1, -1):
        part = forward[k]
        for i in range(k + 1, NBLK):
            part = part - dot_nn(backward[i], read_block(a_ref, place_of(i, k)), HIGH)
        backward[k] = dot_nn(part, w_ref[k], HIGH)
    coef = jnp.concatenate(backward, axis=1)
    coef_ref[...] = coef
    score_ref[...] = dot_nt(coef.astype(BF16), fix_ref[...]) + member_ref[...]


def device_sum(value):
    for axes, size in ((("y", "core"), 8), (("z", "x"), 16)):
        spread = jnp.broadcast_to(value[None], (size,) + value.shape)
        value = jnp.sum(lax.all_to_all(spread, axes, split_axis=0, concat_axis=0, tiled=True), axis=0)
    return value


def shards(fixed_rows, member_rows, target, fixed_prev, member_id):
    count = fixed_rows.shape[0]
    devices = lax.axis_size(ALL)
    cap = 3 * count // devices
    slots = devices * cap
    core = lax.axis_index("core")
    swap = [(0, 1), (1, 0)]
    other = lax.ppermute(fixed_rows, "core", swap)

    target_row = target.reshape(1, count)
    send, slot = pl.pallas_call(
        functools.partial(dispatch_kernel, cap),
        out_shape=(
            jax.ShapeDtypeStruct((slots, PAY), BF16),
            jax.ShapeDtypeStruct((1, count), jnp.int32),
        ),
        compiler_params=params(),
        name="dispatch",
    )(fixed_rows, fixed_prev.reshape(1, FIX), target_row, member_id.reshape(1, count), member_rows)
    recv = lax.all_to_all(send.reshape(devices, cap, PAY), ALL, split_axis=0, concat_axis=0, tiled=True)

    table = jnp.array(pair_table(), jnp.int32)[core]
    gram = gram_blocks(fixed_rows, other, table[:, 0], table[:, 1])
    shares = lax.all_to_all(gram, CHIPS, split_axis=0, concat_axis=0, tiled=True)
    share = jnp.sum(shares, axis=0)
    whole = lax.all_gather(share, ALL, axis=0, tiled=False)
    whole = whole.reshape(devices // 2, 2, CORE_PAIRS, 8, 128)

    member_coef, slot_score = pl.pallas_call(
        member_kernel,
        out_shape=(
            jax.ShapeDtypeStruct((MEM_DEV, MEM), F32),
            jax.ShapeDtypeStruct((1, slots), F32),
        ),
        scratch_shapes=[
            pltpu.VMEM((PAY, slots), BF16),
            pltpu.VMEM((MEM_DEV, MEM, MEM), F32),
            pltpu.VMEM((MEM_DEV, MEM), F32),
        ],
        compiler_params=params(),
        name="members",
    )(recv.reshape(slots, PAY))
    back = lax.all_to_all(slot_score.reshape(devices, cap), ALL, split_axis=0, concat_axis=0, tiled=True)
    member_score, fixed_resid = pl.pallas_call(
        combine_kernel,
        out_shape=(
            jax.ShapeDtypeStruct((1, count), F32),
            jax.ShapeDtypeStruct((1, count), BF16),
        ),
        compiler_params=params(),
        name="combine",
    )(back.reshape(1, slots), slot, target_row)
    gradient = device_sum(dot_nn(fixed_resid, fixed_rows))

    lower, inverses = factor_fixed(whole)
    fixed_coef, row_scores = pl.pallas_call(
        solve_kernel,
        out_shape=(
            jax.ShapeDtypeStruct((1, FIX), F32),
            jax.ShapeDtypeStruct((1, count), F32),
        ),
        compiler_params=params(),
        name="substitute",
    )(lower, inverses, gradient, fixed_rows, member_score)
    return (fixed_coef.reshape(FIX), member_coef, row_scores.reshape(count))


def solution(mesh):
    grid = Mesh(mesh.devices.reshape(4, 4, 4, 2), ALL)
    placed = (P(ALL, None), P(ALL, None), P(ALL), P(), P(ALL))
    return jax.shard_map(
        shards,
        mesh=grid,
        in_specs=placed,
        out_specs=(P(), P(ALL, None), P(ALL)),
        check_vma=False,
    )
```

time: 1910 us -> 428 us (0.22)
  other arithmetic: 750 us -> 6.13 us
  waiting for transfers between devices: 716 us -> 6.46 us
  Pallas kernels: 0 us -> 244 us
  matrix products: 174 us -> 2.86 us
  local copies, waits for them, and re-layouts: 138 us -> 4.88 us
  blocking collectives: 62.8 us -> 141 us
  starting transfers between devices: 27.8 us -> 1.54 us
    another operation x84 -> x0, other arithmetic: 727 us -> none  [the longest x69 474 us: block_solve(): factor_blk = jnp.linalg.cholesky(work[lo:hi, lo:hi])]
    reduce_scatter x1 -> x0, waiting for transfers between devices: 662 us -> none  [shards(): lax.psum_scatter(lax.dot_general(fixed_rows, fixed_rows, (((0,), (0,)), (...]
    pallas_call x0 -> x6, Pallas kernels: none -> 244 us  [the longest x1 141 us: factor_fixed(): pl.pallas_call(factor_kernel, out_shape=(jax.ShapeDtypeStruct((count, 64,...]
    all_to_all x0 -> x5, blocking collectives: none -> 141 us  [the longest x1 68.3 us: shards(): lax.all_to_all(gram, CHIPS, split_axis=0, concat_axis=0, tiled=True)]
    dot_general x34 -> x1, matrix products: 87.8 us -> 2.86 us  [dot_nn(): lax.dot_general(a, b, (((1,), (0,)), ((), ())), precision=precision, pref...]
    another operation x57 -> x0, matrix products: 71.1 us -> none  [the longest x31 36.2 us: block_solve(): jax.scipy.linalg.solve_triangular(factor_blk, eye_block, lower=True)]
    another operation x81 -> x0, local copies, waits for them, and re-layouts: 66 us -> none  [the longest x55 52 us: block_solve(): jax.scipy.linalg.solve_triangular(factor_blk, eye_block, lower=True)]
    psum x1 -> x0, blocking collectives: 62.8 us -> none  [shards(): lax.psum(jnp.dot(fixed_resid, fixed_rows, preferred_element_type=jnp.floa...]
  transfers between devices with their start and end apart: 6 -> 2, of which waited for: 5 -> 1; matrix products, arithmetic and copies ran while one was open for 15% -> 2% of each run, Pallas kernels for 0% -> 15%
where the time goes in v1:
time: 428 us; the launch traced here: 421 us
  Pallas kernels  244 us (57%)
  blocking collectives  141 us (33%)
  between operations  14.5 us (3%)
  waiting for transfers between devices  6.46 us (2%)
  other arithmetic  6.13 us (1%)
  local copies, waits for them, and re-layouts  4.88 us (1%)
    pallas_call x1, Pallas kernels, factor_fixed(): pl.pallas_call(factor_kernel, out_shape=(jax.ShapeDtypeStruct((count, 64,...  141 us
    all_to_all x1, blocking collectives, shards(): lax.all_to_all(gram, CHIPS, split_axis=0, concat_axis=0, tiled=True)  68.3 us
    pallas_call x1, Pallas kernels, shards(): pl.pallas_call(member_kernel, out_shape=(jax.ShapeDtypeStruct((MEM_DEV, M...  51.2 us
    all_to_all x1, blocking collectives, shards(): lax.all_to_all(send.reshape(devices, cap, PAY), ALL, split_axis=0, concat...  40.7 us
    pallas_call x1, Pallas kernels, shards(): pl.pallas_call(solve_kernel, out_shape=(jax.ShapeDtypeStruct((1, FIX), F3...  22.6 us
    all_to_all x2, blocking collectives, device_sum(): lax.all_to_all(spread, axes, split_axis=0, concat_axis=0, tiled=True)  17.8 us
    pallas_call x1, Pallas kernels, gram_blocks(): pl.pallas_call(gram_kernel, out_shape=jax.ShapeDtypeStruct((64, CORE_PAIR...  17.6 us
    all_to_all x1, blocking collectives, shards(): lax.all_to_all(slot_score.reshape(devices, cap), ALL, split_axis=0, conca...  14.4 us
  transfers between devices with their start and end apart: 2, of which 1 were waited for; matrix products, arithmetic and copies ran while one was open for 2% of the time, Pallas kernels for 15%

profile of v1, /device:TPU:1, one launch (start us, length us, event | category | flops | bytes accessed | tf_op | source)
XLA Modules:
  0.0 421.2 jit_solution(12347068510022371997)
XLA Ops:
  7.2 0.0 all-gather.3.cloned.1.call-start
  7.2 1.5 collective-permute-start
  8.7 0.7 dynamic-slice_bitcast_fusion
  9.4 6.4 %collective-permute-done.other_i.other_j = bf16[1024,2048]{1,0:T(8,128)(2,1)} collective-permute-done((bf16[1024,2048]{1,0:T(8,128)(2,1)}, bf16[1024,2048]{1,0:T(8,128)(2,1)}, u32[]{:S(2)}, u32[]{:S(2)}) %collective-permute-start) | collective-permute-done | bytes 4194336 | tf_op jit(solution)/shard_map/ppermute | solution.py:372
  15.8 0.0 copy-start
  15.8 2.2 copy-done
  18.0 17.6 %gram.1 = f32[64,18,8,128]{3,2,1,0:T(8,128)S(1)} custom-call(s32[18]{0:T(128)S(1)} %get-tuple-element.24.hi_ref, s32[18]{0:T(128)S(1)} %get-tuple-element.23.lo_ref, bf16[1024,2048]{1,0:T(8,128)(2,1)S(1)} %copy-done, bf16[1024,2048]{1,0:T(8,128)(2,1)S(1)} %copy-done, bf16[1024,2048]{1,0:T(8,128)(2,1)} %collective-permute-done.other_i.other_j, ...), custom_call_target="tpu_custom_call" | custom-call | tf_op jit(solution)/shard_map/gram/pallas_call | solution.py:228
  35.6 68.3 %all_to_all.29 = f32[64,18,8,128]{3,2,1,0:T(8,128)} all-to-all(f32[64,18,8,128]{3,2,1,0:T(8,128)S(1)} %gram.1), channel_id=1, replica_groups=mesh['z'=4,'x'=4,'y'=4,'core'=2] {'z','x','y'}, dimensions={0} | all-to-all | bytes 9437184 | tf_op jit(solution)/shard_map/all_to_all | solution.py:388
  103.9 0.0 copy-start.1
  103.9 3.2 reduce_sum.29
  107.1 0.0 all-gather.3.cloned.1.call-update
  107.1 0.0 copy-done.1
  107.1 0.6 reshape.53.prev_ref
  107.7 8.8 %dispatch.1 = (bf16[3072,384]{1,0:T(8,128)(2,1)}, s32[1,1024]{1,0:T(1,128)}) custom-call(bf16[1024,2048]{1,0:T(8,128)(2,1)} %fix_ref.3, bf16[1,2048]{1,0:T(2,128)(2,1)} %reshape.53.prev_ref, f32[1,1024]{1,0:T(1,128)} %bitcast.26, s32[1,1024]{1,0:T(1,128)} %bitcast.28, bf16[1024,256]{1,0:T(8,128)(2,1)} %rows_ref.1), custom_call_target="tpu_custom_call" | custom-call | tf_op jit(solution)/shard_map/dispatch/pallas_call | solution.py:375
  116.6 40.7 %all_to_all.30 = bf16[128,24,384]{2,1,0:T(8,128)(2,1)} all-to-all(bf16[128,24,384]{2,1,0:T(8,128)(2,1)} %bitcast.22), channel_id=1, replica_groups=mesh['z'=4,'x'=4,'y'=4,'core'=2] {'z','x','y','core'}, dimensions={0} | all-to-all | bytes 4718592 | tf_op jit(solution)/shard_map/all_to_all | solution.py:384
  157.3 51.2 %members.1 = (f32[4,256]{1,0:T(4,128)}, f32[1,3072]{1,0:T(1,128)}) custom-call(bf16[3072,384]{1,0:T(8,128)(2,1)} %bitcast.21), custom_call_target="tpu_custom_call" | custom-call | tf_op jit(solution)/shard_map/members/pallas_call | solution.py:393
  208.5 0.5 broadcast.10
  209.0 1.4 reduce.8
  210.4 0.1 all_to_all.20
  210.5 14.4 %all_to_all.31 = f32[128,1,24]{2,1,0:T(1,128)S(1)} all-to-all(f32[128,1,24]{2,1,0:T(1,128)S(1)} %bitcast.23), channel_id=1, replica_groups=mesh['z'=4,'x'=4,'y'=4,'core'=2] {'z','x','y','core'}, dimensions={0} | all-to-all | bytes 24576 | tf_op jit(solution)/shard_map/all_to_all | solution.py:407
  224.9 0.8 reduce.9
  225.7 0.7 reshape.58.back_ref
  226.4 2.4 combine.1
  228.8 2.9 fusion
  231.7 8.0 %all_to_all.32 = f32[8,1,2048]{2,1,0:T(1,128)S(1)} all-to-all(f32[8,1,2048]{2,1,0:T(1,128)S(1)} %broadcast_in_dim.4), channel_id=1, replica_groups=mesh['z'=4,'x'=4,'y'=4,'core'=2] {'y','core'}, dimensions={0} | all-to-all | bytes 131072 | tf_op jit(solution)/shard_map/all_to_all | solution.py:361
  239.7 0.1 reduce_sum.30
  239.8 0.1 broadcast_in_dim.5
  239.8 9.8 %all_to_all.33 = f32[16,1,2048]{2,1,0:T(1,128)S(1)} all-to-all(f32[16,1,2048]{2,1,0:T(1,128)S(1)} %broadcast_in_dim.5), channel_id=1, replica_groups=mesh['z'=4,'x'=4,'y'=4,'core'=2] {'z','x'}, dimensions={0} | all-to-all | bytes 262144 | tf_op jit(solution)/shard_map/all_to_all | solution.py:361
  249.7 0.7 reduce_sum.31
  250.3 0.0 all-gather.3.cloned.1.call-done
  250.3 141.0 %factor_fixed.1 = (f32[36,64,8,128]{3,2,1,0:T(8,128)}, f32[8,256,256]{2,1,0:T(8,128)}) custom-call(f32[64,2,18,8,128]{4,3,2,1,0:T(8,128)} %bitcast.20), custom_call_target="tpu_custom_call" | custom-call | tf_op jit(solution)/shard_map/factor_fixed/pallas_call | solution.py:319
  391.3 22.6 %substitute.1 = (f32[1,2048]{1,0:T(1,128)}, f32[1,1024]{1,0:T(1,128)}) custom-call(f32[36,64,8,128]{3,2,1,0:T(8,128)} %get-tuple-element.13.a_ref, f32[8,256,256]{2,1,0:T(8,128)} %get-tuple-element.14.w_ref, f32[1,2048]{1,0:T(1,128)} %bitcast.24, bf16[1024,2048]{1,0:T(8,128)(2,1)} %fix_ref.3, f32[1,1024]{1,0:T(1,128)} %get-tuple-element.19.member_ref), custom_call_target="tpu_custom_call" | custom-call | tf_op jit(solution)/shard_map/substitute/pallas_call | solution.py:420
  (2 shorter events, 0.0 us)
Async XLA Ops:
  7.2 243.2 %all-gather.3.cloned.1.call-start = ((), (), s32[]{:S(2)}) async-start(), calls=%async_computation.5 | async-start | bytes 9510912 | tf_op jit(solution)/shard_map/all_gather | solution.py:390
  7.2 8.6 %collective-permute-start = (bf16[1024,2048]{1,0:T(8,128)(2,1)}, bf16[1024,2048]{1,0:T(8,128)(2,1)}, u32[]{:S(2)}, u32[]{:S(2)}) collective-permute-start(bf16[1024,2048]{1,0:T(8,128)(2,1)} %fix_ref.3), channel_id=1, source_target_pairs={{0,1},{1,0},{2,3},{3,2},{4,5},{5,4},{6,7},{7,6},{8,9},{9,8},{10,11... | collective-permute-start | bytes 12582920 | tf_op jit(solution)/shard_map/ppermute | solution.py:372
  15.8 2.2 copy-start
  103.9 3.2 copy-start.1
Sparse Core Ops, SparseCore 0:
  107.2 81.6 all-gather.2

commit v2 on v1

--- a/solution.py
+++ b/solution.py
@@ -17,7 +17,6 @@
 MEM_DEV = 4
 RIDGE_FIXED = 4.0
 RIDGE_MEMBER = 1.0
-GROUP = 1
 
 FIX = 2048
 MEM = 256
@@ -34,7 +33,7 @@
         for i in range(4 * core, 4 * core + 4):
             pairs += [(i, (i + k) % NBLK) for k in range(4)]
         pairs += [(0, 4), (1, 5)] if core == 0 else [(6, 2), (7, 3)]
-        table.append([(max(p), min(p)) for p in pairs])
+        table.append(sorted((max(p), min(p)) for p in pairs))
     return table
 
 
@@ -52,6 +51,10 @@
 
 def dot_tn(a, b, precision=None):
     return lax.dot_general(a, b, (((0,), (0,)), ((), ())), precision=precision, preferred_element_type=F32)
+
+
+def cost(us):
+    return pl.CostEstimate(flops=int(us * 1e9), transcendentals=0, bytes_accessed=int(us * 2e6))
 
 
 def split3(v):
@@ -60,6 +63,24 @@
     mid = rest.astype(BF16)
     low = (rest - mid.astype(F32)).astype(BF16)
     return hi, mid, low
+
+
+def as_left(v, axis):
+    h, m, l = split3(v)
+    return jnp.concatenate([h, h, m, h, l, m], axis=axis)
+
+
+def as_right(v, axis):
+    h, m, l = split3(v)
+    return jnp.concatenate([h, m, h, l, h, m], axis=axis)
+
+
+def full_nn(a, b):
+    return dot_nn(as_left(a, 1), as_right(b, 0))
+
+
+def full_nt(a, b):
+    return dot_nt(as_left(a, 1), as_right(b, 1))
 
 
 def over_lanes(v, c):
@@ -117,7 +138,8 @@
                 a[p][s + 1], e[p][s + 1] = r1[p], f1[p]
                 b[p] = bn[p]
             if s < 14:
-                u = dot_tn(y, jnp.concatenate([y, z], axis=1), HIGH)
+                both = jnp.concatenate([y, z], axis=1)
+                u = dot_tn(as_left(y, 0), as_right(both, 0))
                 for t in range(s + 2, 16):
                     a[p][t] = a[p][t] - u[8 * t : 8 * t + 8, :128]
                     e[p][t] = e[p][t] - u[8 * t : 8 * t + 8, 128:]
@@ -179,22 +201,17 @@
     for m in range(MEM_DEV):
         gram_ref[m] = dot_nn(turned_ref[:MEM, :] * hots[m : m + 1, :], rows) + ridge
 
-    def solve(p, carry):
-        base = GROUP * p
-        grams = [gram_ref[base + i] for i in range(GROUP)]
-        w0 = factor128([g[:128, :128] for g in grams])
-        l10 = [dot_nt(g[128:, :128], w, HIGH) for g, w in zip(grams, w0)]
-        w1 = factor128([g[128:, 128:] - dot_nt(l, l, HIGH) for g, l in zip(grams, l10)])
-        for i in range(GROUP):
-            right = rhs_ref[pl.ds(base + i, 1), :]
-            y0 = dot_nt(right[:, :128], w0[i], HIGH)
-            y1 = dot_nt(right[:, 128:] - dot_nt(y0, l10[i], HIGH), w1[i], HIGH)
-            x1 = dot_nn(y1, w1[i], HIGH)
-            x0 = dot_nn(y0 - dot_nn(x1, l10[i], HIGH), w0[i], HIGH)
-            coef_ref[pl.ds(base + i, 1), :] = jnp.concatenate([x0, x1], axis=1)
-        return carry
-
-    lax.fori_loop(0, MEM_DEV // GROUP, solve, 0)
+    grams = [gram_ref[m] for m in range(MEM_DEV)]
+    w0 = factor128([g[:128, :128] for g in grams])
+    l10 = [full_nt(g[128:, :128], w) for g, w in zip(grams, w0)]
+    w1 = factor128([g[128:, 128:] - full_nt(l, l) for g, l in zip(grams, l10)])
+    for m in range(MEM_DEV):
+        right = rhs_ref[m : m + 1, :]
+        y0 = full_nt(right[:, :128], w0[m])
+        y1 = full_nt(right[:, 128:] - full_nt(y0, l10[m]), w1[m])
+        x1 = full_nn(y1, w1[m])
+        x0 = full_nn(y0 - full_nn(x1, l10[m]), w0[m])
+        coef_ref[m : m + 1, :] = jnp.concatenate([x0, x1], axis=1)
     low = coef_ref[...].astype(BF16)
     projected = dot_nn(low, turned_ref[:MEM, :])
     score_ref[...] = jnp.sum(projected * hots.astype(F32), axis=0, keepdims=True)
@@ -216,8 +233,15 @@
     resid_ref[...] = (target_ref[...] - score).astype(BF16)
 
 
-def gram_kernel(hi_ref, lo_ref, own_i, own_j, other_i, other_j, out_ref):
-    block = dot_tn(own_i[...], own_j[...]) + dot_tn(other_i[...], other_j[...])
+def gram_kernel(hi_ref, lo_ref, own_i, own_j, other_i, other_j, out_ref, turned_ref):
+    b = pl.program_id(0)
+
+    @pl.when((b == 0) | (hi_ref[b] != hi_ref[jnp.maximum(b - 1, 0)]))
+    def _():
+        turned_ref[0] = own_i[...].T
+        turned_ref[1] = other_i[...].T
+
+    block = dot_nn(turned_ref[0], own_j[...]) + dot_nn(turned_ref[1], other_j[...])
     out_ref[:32, 0] = block[:, :128].reshape(32, 8, 128)
     out_ref[32:, 0] = block[:, 128:].reshape(32, 8, 128)
 
@@ -238,9 +262,11 @@
                 tall(lambda b, hi, lo: (0, lo[b])),
             ],
             out_specs=pl.BlockSpec((64, 1, 8, 128), lambda b, hi, lo: (0, b, 0, 0)),
-        ),
-        compiler_params=params(32),
+            scratch_shapes=[pltpu.VMEM((2, BLK, rows), BF16)],
+        ),
+        compiler_params=params(),
         name="gram",
+        cost_estimate=cost(10),
     )(hi, lo, own, own, other, other)
 
 
@@ -257,7 +283,7 @@
     a_ref[at] = jnp.concatenate([value[:, :128], value[:, 128:]], axis=0).reshape(64, 8, 128)
 
 
-def factor_kernel(gram_ref, a_ref, w_ref, left_ref, right_ref, sems):
+def factor_kernel(gram_ref, a_ref, w_ref, done_ref, left_ref, right_ref, sems):
     copies = []
     for core, pairs in enumerate(pair_table()):
         for b, (i, j) in enumerate(pairs):
@@ -279,18 +305,18 @@
     def step(k, carry):
         diag = a_ref[place_of(k, k)].reshape(2 * BLK, 128)
         w00 = factor128([diag[:128] + ridge])[0]
-        l10 = dot_nt(diag[128:256], w00, HIGH)
-        w11 = factor128([diag[384:] + ridge - dot_nt(l10, l10, HIGH)])[0]
-        w10 = -dot_nn(w11, dot_nn(l10, w00, HIGH), HIGH)
+        l10 = full_nt(diag[128:256], w00)
+        w11 = factor128([diag[384:] + ridge - full_nt(l10, l10)])[0]
+        w10 = -full_nn(w11, full_nn(l10, w00))
         w_ref[k, :128, :128] = w00
         w_ref[k, :128, 128:] = jnp.zeros((128, 128), F32)
         w_ref[k, 128:, :128] = w10
         w_ref[k, 128:, 128:] = w11
-        whole = w_ref[k]
+        whole = as_right(w_ref[k], 1)
 
         def panel(i, carry):
             at = place_of(i, k)
-            value = dot_nt(read_block(a_ref, at), whole, HIGH)
+            value = dot_nt(as_left(read_block(a_ref, at), 1), whole)
             write_block(a_ref, at, value)
             h, m, l = split3(value)
             left_ref[i] = jnp.concatenate([h, h, m, h, l, m], axis=1)
@@ -312,6 +338,7 @@
         return lax.fori_loop(k + 1, NBLK, trail_row, carry)
 
     lax.fori_loop(0, NBLK, step, 0)
+    done_ref[...] = jnp.zeros((8, 128), F32)
 
 
 def factor_fixed(gram):
@@ -321,9 +348,11 @@
         out_shape=(
             jax.ShapeDtypeStruct((count, 64, 8, 128), F32),
             jax.ShapeDtypeStruct((NBLK, BLK, BLK), F32),
+            jax.ShapeDtypeStruct((8, 128), F32),
         ),
         in_specs=[pl.BlockSpec(memory_space=pl.ANY)],
         out_specs=(
+            pl.BlockSpec(memory_space=pltpu.VMEM),
             pl.BlockSpec(memory_space=pltpu.VMEM),
             pl.BlockSpec(memory_space=pltpu.VMEM),
         ),
@@ -332,34 +361,52 @@
             pltpu.VMEM((NBLK, BLK, 6 * BLK), BF16),
             pltpu.SemaphoreType.DMA((count,)),
         ],
-        compiler_params=params(),
+        compiler_params=params(44),
         name="factor_fixed",
+        cost_estimate=cost(100),
     )(gram)
 
 
+def halves(a_ref, at):
+    flat = a_ref[at].reshape(2 * BLK, 128)
+    return flat[:BLK], flat[BLK:]
+
+
 def solve_kernel(a_ref, w_ref, grad_ref, fix_ref, member_ref, coef_ref, score_ref):
+    turned = [w_ref[k].T for k in range(NBLK)]
+
+    def times_row(left, right, row):
+        return left * row[:, :128] + right * row[:, 128:]
+
+    def as_column(spread):
+        return jnp.sum(spread, axis=1, keepdims=True)
+
     forward = []
     for k in range(NBLK):
-        part = grad_ref[:, BLK * k : BLK * k + BLK]
-        for j in range(k):
-            part = part - dot_nt(forward[j], read_block(a_ref, place_of(k, j)), HIGH)
-        forward.append(dot_nt(part, w_ref[k], HIGH))
+        part = grad_ref[:, BLK * k : BLK * k + BLK].T
+        if k:
+            total = jnp.zeros((BLK, 128), F32)
+            for j in range(k):
+                left, right = halves(a_ref, place_of(k, j))
+                total = total + times_row(left, right, forward[j])
+            part = part - as_column(total)
+        forward.append(jnp.sum(turned[k] * part, axis=0, keepdims=True))
     backward = [None] * NBLK
     for k in range(NBLK - 1, -1, -1):
         part = forward[k]
-        for i in range(k + 1, NBLK):
-            part = part - dot_nn(backward[i], read_block(a_ref, place_of(i, k)), HIGH)
-        backward[k] = dot_nn(part, w_ref[k], HIGH)
-    coef = jnp.concatenate(backward, axis=1)
+        if k + 1 < NBLK:
+            total = [jnp.zeros((8, 128), F32) for _ in range(2)]
+            for i in range(k + 1, NBLK):
+                for h, piece in enumerate(halves(a_ref, place_of(i, k))):
+                    gain = (piece * backward[i]).reshape(BLK // 8, 8, 128)
+                    total[h] = total[h] + jnp.sum(gain, axis=0)
+            part = part - jnp.concatenate(
+                [jnp.sum(total[h], axis=0, keepdims=True) for h in range(2)], axis=1
+            )
+        backward[k] = as_column(times_row(turned[k][:, :128], turned[k][:, 128:], part))
+    coef = jnp.concatenate([jnp.broadcast_to(x, (BLK, 128)).T[:1] for x in backward], axis=1)
     coef_ref[...] = coef
     score_ref[...] = dot_nt(coef.astype(BF16), fix_ref[...]) + member_ref[...]
-
-
-def device_sum(value):
-    for axes, size in ((("y", "core"), 8), (("z", "x"), 16)):
-        spread = jnp.broadcast_to(value[None], (size,) + value.shape)
-        value = jnp.sum(lax.all_to_all(spread, axes, split_axis=0, concat_axis=0, tiled=True), axis=0)
-    return value
 
 
 def shards(fixed_rows, member_rows, target, fixed_prev, member_id):
@@ -380,12 +427,15 @@
         ),
         compiler_params=params(),
         name="dispatch",
+        cost_estimate=cost(9),
     )(fixed_rows, fixed_prev.reshape(1, FIX), target_row, member_id.reshape(1, count), member_rows)
-    recv = lax.all_to_all(send.reshape(devices, cap, PAY), ALL, split_axis=0, concat_axis=0, tiled=True)
+    other, send = lax.optimization_barrier((other, send))
 
     table = jnp.array(pair_table(), jnp.int32)[core]
     gram = gram_blocks(fixed_rows, other, table[:, 0], table[:, 1])
     shares = lax.all_to_all(gram, CHIPS, split_axis=0, concat_axis=0, tiled=True)
+    shares, send = lax.optimization_barrier((shares, send))
+    recv = lax.all_to_all(send.reshape(devices, cap, PAY), ALL, split_axis=0, concat_axis=0, tiled=True)
     share = jnp.sum(shares, axis=0)
     whole = lax.all_gather(share, ALL, axis=0, tiled=False)
     whole = whole.reshape(devices // 2, 2, CORE_PAIRS, 8, 128)
@@ -403,6 +453,7 @@
         ],
         compiler_params=params(),
         name="members",
+        cost_estimate=cost(30),
     )(recv.reshape(slots, PAY))
     back = lax.all_to_all(slot_score.reshape(devices, cap), ALL, split_axis=0, concat_axis=0, tiled=True)
     member_score, fixed_resid = pl.pallas_call(
@@ -413,18 +464,24 @@
         ),
         compiler_params=params(),
         name="combine",
+        cost_estimate=cost(3),
     )(back.reshape(1, slots), slot, target_row)
-    gradient = device_sum(dot_nn(fixed_resid, fixed_rows))
-
-    lower, inverses = factor_fixed(whole)
+    gradient = dot_nn(fixed_resid, fixed_rows)
+    spread = jnp.broadcast_to(gradient[None], (devices, 1, FIX))
+    gradients = lax.all_to_all(spread, ALL, split_axis=0, concat_axis=0, tiled=True)
+
+    lower, inverses, done = factor_fixed(whole)
+    gradients, done = lax.optimization_barrier((gradients, done))
+    gradient = jnp.sum(gradients, axis=0)
     fixed_coef, row_scores = pl.pallas_call(
         solve_kernel,
         out_shape=(
             jax.ShapeDtypeStruct((1, FIX), F32),
             jax.ShapeDtypeStruct((1, count), F32),
         ),
-        compiler_params=params(),
+        compiler_params=params(24),
         name="substitute",
+        cost_estimate=cost(12),
     )(lower, inverses, gradient, fixed_rows, member_score)
     return (fixed_coef.reshape(FIX), member_coef, row_scores.reshape(count))
 

time: 428 us -> 349 us (0.82); the launches traced: 421 us -> 348 us
  Pallas kernels: 244 us -> 172 us
  waiting for transfers between devices: 6.46 us -> 0.03 us
    pallas_call x1, Pallas kernels: 51.2 us -> 21.7 us  [shards(): pl.pallas_call(member_kernel, out_shape=(jax.ShapeDtypeStruct((MEM_DEV, M...]
    pallas_call x1, Pallas kernels: 141 us -> 113 us  [factor_fixed(): pl.pallas_call(factor_kernel, out_shape=(jax.ShapeDtypeStruct((count, 64,...]
    pallas_call x1, Pallas kernels: 22.6 us -> 5.5 us  [shards(): pl.pallas_call(solve_kernel, out_shape=(jax.ShapeDtypeStruct((1, FIX), F3...]
    ppermute x1, waiting for transfers between devices: 6.44 us -> 0.01 us  [shards(): other = lax.ppermute(fixed_rows, 'core', swap)]
    all_to_all x2 -> x1, blocking collectives: 17.8 us -> 23.1 us  [shards(): lax.all_to_all(spread, ALL, split_axis=0, concat_axis=0, tiled=True)]
  transfers between devices with their start and end apart: 2 -> 2, of which waited for: 1 -> 0; matrix products, arithmetic and copies ran while one was open for 2% -> 2% of each run, Pallas kernels for 15% -> 9%
where the time goes in v2:
time: 349 us; the launch traced here: 348 us
  Pallas kernels  172 us (49%)
  blocking collectives  145 us (42%)
  between operations  14.1 us (4%)
  local copies, waits for them, and re-layouts  8.03 us (2%)
  other arithmetic  6.19 us (2%)
    pallas_call x1, Pallas kernels, factor_fixed(): pl.pallas_call(factor_kernel, out_shape=(jax.ShapeDtypeStruct((count, 64,...  113 us
    all_to_all x1, blocking collectives, shards(): lax.all_to_all(gram, CHIPS, split_axis=0, concat_axis=0, tiled=True)  67.7 us
    all_to_all x1, blocking collectives, shards(): lax.all_to_all(send.reshape(devices, cap, PAY), ALL, split_axis=0, concat...  40.6 us
    all_to_all x1, blocking collectives, shards(): lax.all_to_all(spread, ALL, split_axis=0, concat_axis=0, tiled=True)  23.1 us
    pallas_call x1, Pallas kernels, shards(): pl.pallas_call(member_kernel, out_shape=(jax.ShapeDtypeStruct((MEM_DEV, M...  21.7 us
    pallas_call x1, Pallas kernels, gram_blocks(): pl.pallas_call(gram_kernel, out_shape=jax.ShapeDtypeStruct((64, CORE_PAIR...  20.4 us
    all_to_all x1, blocking collectives, shards(): lax.all_to_all(slot_score.reshape(devices, cap), ALL, split_axis=0, conca...  13.8 us
    pallas_call x1, Pallas kernels, shards(): pl.pallas_call(functools.partial(dispatch_kernel, cap), out_shape=(jax.Sh...  8.74 us
  transfers between devices with their start and end apart: 2, of which 0 were waited for; matrix products, arithmetic and copies ran while one was open for 2% of the time, Pallas kernels for 9%

profile of v2, /device:TPU:1, one launch (start us, length us, event | category | flops | bytes accessed | tf_op | source)
XLA Modules:
  0.0 347.9 jit_solution(6426097654661200183)
XLA Ops:
  7.2 0.0 all-gather.3.cloned.1.call-start
  7.2 1.5 collective-permute-start
  8.7 1.3 reshape.47.prev_ref
  10.0 0.7 dynamic-slice_bitcast_fusion
  10.7 0.5 slice_bitcast_fusion
  11.2 8.7 %dispatch.1 = (bf16[3072,384]{1,0:T(8,128)(2,1)}, s32[1,1024]{1,0:T(1,128)}) custom-call(bf16[1024,2048]{1,0:T(8,128)(2,1)} %fix_ref.3, bf16[1,2048]{1,0:T(2,128)(2,1)} %reshape.47.prev_ref, f32[1,1024]{1,0:T(1,128)} %bitcast.27, s32[1,1024]{1,0:T(1,128)} %bitcast.26, bf16[1024,256]{1,0:T(8,128)(2,1)} %rows_ref.1), custom_call_target="tpu_custom_call" | custom-call | flops 8999999488 | bytes 18000000 | tf_op jit(solution)/shard_map/dispatch/pallas_call | solution.py:422
  20.0 0.0 collective-permute-done.other_i.other_j
  20.0 20.4 %gram.1 = f32[64,18,8,128]{3,2,1,0:T(8,128)} custom-call(s32[18]{0:T(128)} %get-tuple-element.32.hi_ref, s32[18]{0:T(128)} %get-tuple-element.31.lo_ref, bf16[1024,2048]{1,0:T(8,128)(2,1)} %fix_ref.3, bf16[1024,2048]{1,0:T(8,128)(2,1)} %fix_ref.3, bf16[1024,2048]{1,0:T(8,128)(2,1)} %collective-permute-done.other_i.other_j, ...), custom_call_target="tpu_custom_call" | custom-call | flops 10000000000 | bytes 20000000 | tf_op jit(solution)/shard_map/gram/pallas_call | solution.py:252
  40.3 67.7 %all_to_all.24 = f32[64,18,8,128]{3,2,1,0:T(8,128)} all-to-all(f32[64,18,8,128]{3,2,1,0:T(8,128)} %gram.1), channel_id=1, replica_groups=mesh['z'=4,'x'=4,'y'=4,'core'=2] {'z','x','y'}, dimensions={0} | all-to-all | bytes 9437184 | tf_op jit(solution)/shard_map/all_to_all | solution.py:436
  108.1 0.0 copy-start.4
  108.1 3.3 reduce_sum.20
  111.4 0.0 all-gather.3.cloned.1.call-update
  111.4 0.0 copy-done.4
  111.4 40.6 %all_to_all.25 = bf16[128,24,384]{2,1,0:T(8,128)(2,1)} all-to-all(bf16[128,24,384]{2,1,0:T(8,128)(2,1)S(1)} %bitcast.21), channel_id=1, replica_groups=mesh['z'=4,'x'=4,'y'=4,'core'=2] {'z','x','y','core'}, dimensions={0} | all-to-all | bytes 4718592 | tf_op jit(solution)/shard_map/all_to_all | solution.py:438
  152.0 21.7 %members.1 = (f32[4,256]{1,0:T(4,128)}, f32[1,3072]{1,0:T(1,128)}) custom-call(bf16[3072,384]{1,0:T(8,128)(2,1)} %bitcast.22), custom_call_target="tpu_custom_call" | custom-call | flops 30000001024 | bytes 60000000 | tf_op jit(solution)/shard_map/members/pallas_call | solution.py:443
  173.7 0.5 broadcast.8
  174.2 1.4 reduce.7
  175.6 0.1 all_to_all.17
  175.7 13.8 %all_to_all.26 = f32[128,1,24]{2,1,0:T(1,128)S(1)} all-to-all(f32[128,1,24]{2,1,0:T(1,128)S(1)} %bitcast.23), channel_id=1, replica_groups=mesh['z'=4,'x'=4,'y'=4,'core'=2] {'z','x','y','core'}, dimensions={0} | all-to-all | bytes 24576 | tf_op jit(solution)/shard_map/all_to_all | solution.py:458
  189.6 0.8 reduce.8
  190.4 0.7 reshape.53.back_ref
  191.1 0.0 copy-start
  191.1 2.5 combine.1
  193.6 0.0 copy-done
  193.6 1.3 fusion
  194.9 0.5 broadcast_in_dim.2
  195.5 23.1 %all_to_all.27 = f32[128,1,2048]{2,1,0:T(1,128)S(1)} all-to-all(f32[128,1,2048]{2,1,0:T(1,128)S(1)} %broadcast_in_dim.2), channel_id=1, replica_groups=mesh['z'=4,'x'=4,'y'=4,'core'=2] {'z','x','y','core'}, dimensions={0} | all-to-all | bytes 2097152 | tf_op jit(solution)/shard_map/all_to_all | solution.py:471
  218.6 0.6 reduce_sum.21
  219.2 0.0 all-gather.3.cloned.1.call-done
  219.2 0.0 copy-start.1
  219.2 0.0 copy-start.3
  219.2 112.7 %factor_fixed.1 = (f32[36,64,8,128]{3,2,1,0:T(8,128)}, f32[8,256,256]{2,1,0:T(8,128)S(1)}, f32[8,128]{1,0:T(8,128)}) custom-call(f32[64,2,18,8,128]{4,3,2,1,0:T(8,128)} %bitcast.25), custom_call_target="tpu_custom_call" | custom-call | flops 99999997952 | bytes 200000000 | tf_op jit(solution)/shard_map/factor_fixed/pallas_call | solution.py:346
  331.9 0.0 copy-done.1
  331.9 0.0 copy-done.3
  331.9 0.0 copy-start.2
  331.9 3.7 %copy-done.2 = f32[36,64,8,128]{3,2,1,0:T(8,128)S(1)} copy-done((f32[36,64,8,128]{3,2,1,0:T(8,128)S(1)}, f32[36,64,8,128]{3,2,1,0:T(8,128)}, u32[]{:S(2)}) %copy-start.2) | copy-done | bytes 9437208
  335.6 5.5 %substitute.1 = (f32[1,2048]{1,0:T(1,128)}, f32[1,1024]{1,0:T(1,128)}) custom-call(f32[36,64,8,128]{3,2,1,0:T(8,128)S(1)} %copy-done.2, f32[8,256,256]{2,1,0:T(8,128)S(1)} %get-tuple-element.22.w_ref, f32[1,2048]{1,0:T(1,128)S(1)} %bitcast.20, bf16[1024,2048]{1,0:T(8,128)(2,1)S(1)} %copy-done.1, f32[1,1024]{1,0:T(1,128)S(1)} %copy-done.3), custom_call_target="tpu_custom_call" | custom-call | flops 12000000000 | bytes 24000000 | tf_op jit(solution)/shard_map/substitute/pallas_call | solution.py:476
Async XLA Ops:
  7.2 212.0 %all-gather.3.cloned.1.call-start = ((), (), s32[]{:S(2)}) async-start(), calls=%async_computation.4 | async-start | bytes 9510912 | tf_op jit(solution)/shard_map/all_gather | solution.py:440
  7.2 12.8 %collective-permute-start = (bf16[1024,2048]{1,0:T(8,128)(2,1)}, bf16[1024,2048]{1,0:T(8,128)(2,1)}, u32[]{:S(2)}, u32[]{:S(2)}) collective-permute-start(bf16[1024,2048]{1,0:T(8,128)(2,1)} %fix_ref.3), channel_id=1, source_target_pairs={{0,1},{1,0},{2,3},{3,2},{4,5},{5,4},{6,7},{7,6},{8,9},{9,8},{10,11... | collective-permute-start | bytes 12582920 | tf_op jit(solution)/shard_map/ppermute | solution.py:419
  108.1 3.4 copy-start.4
  191.1 2.5 copy-start
  219.2 112.7 %copy-start.1 = (bf16[1024,2048]{1,0:T(8,128)(2,1)S(1)}, bf16[1024,2048]{1,0:T(8,128)(2,1)}, u32[]{:S(2)}) copy-start(bf16[1024,2048]{1,0:T(8,128)(2,1)} %fix_ref.3) | copy-start | bytes 12582916
  219.2 112.7 %copy-start.3 = (f32[1,1024]{1,0:T(1,128)S(1)}, f32[1,1024]{1,0:T(1,128)}, u32[]{:S(2)}) copy-start(f32[1,1024]{1,0:T(1,128)} %get-tuple-element.27.member_ref) | copy-start | bytes 12292
  331.9 3.7 %copy-start.2 = (f32[36,64,8,128]{3,2,1,0:T(8,128)S(1)}, f32[36,64,8,128]{3,2,1,0:T(8,128)}, u32[]{:S(2)}) copy-start(f32[36,64,8,128]{3,2,1,0:T(8,128)} %get-tuple-element.21.a_ref) | copy-start | bytes 28311556
Sparse Core Ops, SparseCore 0:
  111.6 83.6 all-gather.2
